TPU v7x, 256 devices: a whole 4x4x8 slice. The times are simulated.
256 devices in a mesh: tile: 128 (over y, z, x), basin: 2 (over core).
Axes of the slice: x: 4, y: 4, z: 8, core: 2. Of those that a mesh axis runs over, the one named last changes fastest.
Arguments:
- cell_features: bfloat16 [65536, 512], P(('tile', 'basin')), may hold values from -6 to 6
- encoded: bfloat16 [1024, 512], P('tile'), may hold values from -6 to 6
- w_query: bfloat16 [512, 512], replicated, may hold values from -0.375 to 0.375
- w_key: bfloat16 [512, 512], replicated, may hold values from -0.375 to 0.375
- w_value: bfloat16 [512, 512], replicated, may hold values from -0.25 to 0.25
- w_out: bfloat16 [512, 512], replicated, may hold values from -0.25 to 0.25
- pattern: int32 [256, 16], P(('tile', 'basin')), may hold values from 0 to 127, all different within a row
- cell_basin: int32 [65536], P(('tile', 'basin')), may hold values from 0 to 511, as said below
- pooled_grad: bfloat16 [512, 512], P(('tile', 'basin')), may hold values from -24 to 24
Outputs:
- pooled: bfloat16 [512, 512], P(('tile', 'basin'))
- grad_cells: bfloat16 [65536, 512], P(('tile', 'basin'))
- grad_gauges: bfloat16 [1024, 512], P('tile')
- grad_query_weight: float32 [512, 512], replicated
- grad_key_weight: float32 [512, 512], replicated
- grad_value_weight: float32 [512, 512], replicated
- grad_out_weight: float32 [512, 512], replicated
Inputs may be any that keep to these rules, and one draw needn't show every extreme that they name: `pattern`: each row names 16 different gauge blocks; every block is named by some row. `cell_basin`: cell c lies in basin (2 * (c // 256) + k) mod 512 for some k with -2 <= k < 4; when c % 256 < 6, k = c % 256 - 2.
All inputs are finite; a program needn't handle non-finite values.
Results may differ from a plain program's by a relative error of at most 0.012.
The roundings to bfloat16 on the way count: a program that leaves them out, or rounds other values in their place, can miss the bound.
Values may be sent and summed in bfloat16 or wider, within the bound.
No kernel may reach another device: no remote copies, remote signals or barrier semaphores. Data moves between devices by JAX's collectives and lax.ppermute only.
A program may use at most 64 MiB of HBM per device.

v0:
```python
import math
import jax
import jax.numpy as jnp
from jax import lax
from jax.sharding import PartitionSpec as P

HEADS = 8
HEAD_DIM = 64
score_cap = 30.0


def shifted(value, axis, steps):
    count = lax.axis_size(axis)
    pairs = [(source, (source + steps) % count) for source in range(count)]
    return lax.ppermute(value, axis, pairs)


def forward_heads(queries, key_sel, value_sel):
    row_count = queries.shape[0]
    key_count = key_sel.shape[0]
    query_heads = queries.reshape(row_count, HEADS, HEAD_DIM)
    key_heads = key_sel.reshape(key_count, HEADS, HEAD_DIM)
    value_heads = value_sel.reshape(key_count, HEADS, HEAD_DIM)
    scores = jnp.einsum(
        "rhd,khd->hrk", query_heads, key_heads, preferred_element_type=jnp.float32
    ) * (1.0 / math.sqrt(HEAD_DIM))
    tanh_val = jnp.tanh(scores / score_cap)
    exponent = jnp.exp(score_cap * tanh_val)
    weights = exponent / jnp.sum(exponent, axis=-1, keepdims=True)
    weights_bf = weights.astype(jnp.bfloat16)
    attended = jnp.einsum(
        "hrk,khd->rhd", weights_bf, value_heads, preferred_element_type=jnp.float32
    )
    attended = attended.reshape(row_count, HEADS * HEAD_DIM).astype(jnp.bfloat16)
    return (attended, weights, weights_bf, tanh_val)


def backward_heads(queries, key_sel, value_sel, weights, weights_bf, tanh_val, attended_grad):
    row_count = queries.shape[0]
    key_count = key_sel.shape[0]
    query_heads = queries.reshape(row_count, HEADS, HEAD_DIM)
    key_heads = key_sel.reshape(key_count, HEADS, HEAD_DIM)
    value_heads = value_sel.reshape(key_count, HEADS, HEAD_DIM)
    grad_heads = attended_grad.reshape(row_count, HEADS, HEAD_DIM)
    weight_grad = jnp.einsum(
        "rhd,khd->hrk", grad_heads, value_heads, preferred_element_type=jnp.float32
    )
    value_grad = jnp.einsum(
        "hrk,rhd->khd", weights_bf, grad_heads, preferred_element_type=jnp.float32
    )
    inner_sum = jnp.sum(weights * weight_grad, axis=-1, keepdims=True)
    score_grad = (
        weights
        * (weight_grad - inner_sum)
        * (1.0 - tanh_val * tanh_val)
        * (1.0 / math.sqrt(HEAD_DIM))
    )
    score_grad = score_grad.astype(jnp.bfloat16)
    query_grad = jnp.einsum(
        "hrk,khd->rhd", score_grad, key_heads, preferred_element_type=jnp.float32
    )
    query_grad = query_grad.reshape(row_count, HEADS * HEAD_DIM).astype(jnp.bfloat16)
    key_grad = jnp.einsum(
        "hrk,rhd->khd", score_grad, query_heads, preferred_element_type=jnp.float32
    )
    return (
        query_grad,
        key_grad.reshape(key_count, HEADS * HEAD_DIM),
        value_grad.reshape(key_count, HEADS * HEAD_DIM),
    )


def fetch_gauges(moving):
    return lax.all_gather(moving, "tile", axis=0, tiled=True)


def sum_cores(partial_value):
    return lax.psum(partial_value, "basin")


def contract_rows(left_side, right_side):
    return lax.dot_general(
        left_side, right_side, (((0,), (0,)), ((), ())), preferred_element_type=jnp.float32
    )


def contract_cols(left_side, right_side):
    return lax.dot_general(
        left_side, right_side, (((1,), (1,)), ((), ())), preferred_element_type=jnp.float32
    )


def per_device(
    cell_features, encoded, w_query, w_key, w_value, w_out, pattern, cell_basin, pooled_grad
):
    highest = lax.Precision.HIGHEST
    cell_count = cell_features.shape[0]
    model_width = cell_features.shape[1]
    gauge_rows = encoded.shape[0]
    chosen_blocks = pattern[0]
    block_count = chosen_blocks.shape[0]
    tile_count = lax.axis_size("tile")
    queries = jnp.dot(cell_features, w_query, preferred_element_type=jnp.float32).astype(
        jnp.bfloat16
    )
    own_keys = jnp.dot(encoded, w_key, preferred_element_type=jnp.float32).astype(jnp.bfloat16)
    own_values = jnp.dot(encoded, w_value, preferred_element_type=jnp.float32).astype(jnp.bfloat16)
    moving = jnp.concatenate([own_keys, own_values], axis=1)
    gathered = fetch_gauges(moving)
    shaped = gathered.reshape(tile_count, gauge_rows, gathered.shape[1])
    picked = jnp.take(shaped, chosen_blocks, axis=0).reshape(
        block_count * gauge_rows, gathered.shape[1]
    )
    key_sel = picked[:, :model_width]
    value_sel = picked[:, model_width:]
    block_rows = min(512, cell_count)
    block_total = cell_count // block_rows
    query_blocks = queries.reshape(block_total, block_rows, model_width)

    def attend_block(query_block):
        return forward_heads(query_block, key_sel, value_sel)[0]

    attended = lax.map(attend_block, query_blocks).reshape(cell_count, model_width)
    cell_out = jnp.dot(attended, w_out, preferred_element_type=jnp.float32).astype(jnp.bfloat16)
    device = lax.axis_index(("tile", "basin"))
    own_basins = pooled_grad.shape[0]
    basin_total = own_basins * lax.axis_size(("tile", "basin"))
    basin_slot = (cell_basin - device * own_basins + own_basins) % basin_total
    slot_count = 3 * own_basins
    onehot = (basin_slot[:, None] == jnp.arange(slot_count, dtype=jnp.int32)[None, :]).astype(
        jnp.bfloat16
    )
    basin_sums = contract_rows(onehot, cell_out)
    slot_counts = jnp.sum(onehot, axis=0, dtype=jnp.float32)
    lower_part = (basin_sums[:own_basins], slot_counts[:own_basins])
    upper_part = (basin_sums[2 * own_basins :], slot_counts[2 * own_basins :])
    from_above = shifted((lower_part[0], lower_part[1]), ("tile", "basin"), -1)
    from_below = shifted((upper_part[0], upper_part[1]), ("tile", "basin"), 1)
    own_sums = basin_sums[own_basins : 2 * own_basins] + from_above[0] + from_below[0]
    own_counts = slot_counts[own_basins : 2 * own_basins] + from_above[1] + from_below[1]
    count_root = jnp.sqrt(own_counts)
    pooled = (own_sums / count_root[:, None]).astype(jnp.bfloat16)
    scaled_table = pooled_grad.astype(jnp.float32) / count_root[:, None]
    below_table = shifted(scaled_table, ("tile", "basin"), 1)
    above_table = shifted(scaled_table, ("tile", "basin"), -1)
    grad_table = jnp.concatenate([below_table, scaled_table, above_table], axis=0)
    out_grad = jnp.take(grad_table, basin_slot, axis=0).astype(jnp.bfloat16)
    grad_out_local = contract_rows(attended, out_grad)
    attended_grad = contract_cols(out_grad, w_out).astype(jnp.bfloat16)
    grad_blocks = attended_grad.reshape(block_total, block_rows, model_width)

    def backward_block(running, pieces):
        query_block, grad_block = pieces
        unused, weights, weights_bf, tanh_val = forward_heads(query_block, key_sel, value_sel)
        query_grad, key_grad, value_grad = backward_heads(
            query_block, key_sel, value_sel, weights, weights_bf, tanh_val, grad_block
        )
        return ((running[0] + key_grad, running[1] + value_grad), query_grad)

    empty = jnp.zeros((key_sel.shape[0], model_width), jnp.float32)
    (key_grad_sel, value_grad_sel), query_grad = lax.scan(
        backward_block, (empty, empty), (query_blocks, grad_blocks)
    )
    query_grad = query_grad.reshape(cell_count, model_width)
    grad_query_local = contract_rows(cell_features, query_grad)
    grad_cells = contract_cols(query_grad, w_query).astype(jnp.bfloat16)
    both_grads = jnp.concatenate([key_grad_sel, value_grad_sel], axis=1)
    both_weights = jnp.concatenate([w_key, w_value], axis=1).astype(jnp.float32)
    column_width = both_grads.shape[1]
    return_term = jnp.zeros((tile_count, gauge_rows, column_width), jnp.float32)
    return_term = return_term.at[chosen_blocks].set(
        both_grads.reshape(block_count, gauge_rows, column_width)
    )
    return_term = return_term.reshape(tile_count * gauge_rows, column_width)
    returned = lax.psum_scatter(return_term, "tile", scatter_dimension=0, tiled=True)
    pair_local = lax.dot_general(
        encoded.astype(jnp.float32), returned, (((0,), (0,)), ((), ())), precision=highest
    )
    partial_value = lax.dot_general(
        returned, both_weights, (((1,), (1,)), ((), ())), precision=highest
    )
    grad_gauges = sum_cores(partial_value)
    grad_gauges = grad_gauges.astype(jnp.bfloat16)
    summed = lax.psum((grad_query_local, grad_out_local, pair_local), ("tile", "basin"))
    grad_query_weight = summed[0]
    grad_out_weight = summed[1]
    grad_key_weight = summed[2][:, :model_width]
    grad_value_weight = summed[2][:, model_width:]
    return (
        pooled,
        grad_cells,
        grad_gauges,
        grad_query_weight,
        grad_key_weight,
        grad_value_weight,
        grad_out_weight,
    )


def solution(mesh):
    return jax.shard_map(
        per_device,
        mesh=mesh,
        in_specs=(
            P(("tile", "basin"), None),
            P("tile", None),
            P(),
            P(),
            P(),
            P(),
            P(("tile", "basin"), None),
            P(("tile", "basin")),
            P(("tile", "basin"), None),
        ),
        out_specs=(
            P(("tile", "basin"), None),
            P(("tile", "basin"), None),
            P("tile", None),
            P(),
            P(),
            P(),
            P(),
        ),
        check_vma=False,
    )
```

profile of v0, /device:TPU:8, one launch (start us, length us, event | category | flops | bytes accessed | tf_op | source)
XLA Modules:
  0.0 1125.6 jit_solution(10916404886895113197)
XLA Ops:
  7.2 1.3 convolution_convert_fusion.6
  8.5 1.2 convolution_convert_fusion.7
  9.8 0.6 pad_maximum_fusion.1
  10.5 0.7 compare_and_fusion
  11.4 7.5 collective-permute-start.2
  18.8 0.7 fusion.31
  19.5 0.7 compare_and_fusion.1
  20.2 1.2 convolution_convert_fusion.5
  21.6 4.6 collective-permute-start.5
  26.4 0.1 copy.41
  26.5 1.0 collective-permute-done.5
  27.5 5.9 collective-permute-done.4
  33.4 1.2 gather_fusion.1
  34.6 0.3 convolution_convert_fusion.2
  35.1 94.1 %all-gather.2.cloned.1.call-done = bf16[1024,1024]{1,0:T(8,128)(2,1)} async-done(((bf16[8,1024]{1,0:T(8,128)(2,1)}), bf16[1024,1024]{1,0:T(8,128)(2,1)}) %all-gather.2.cloned.1.call-update) | async-done | bytes 2097168 | tf_op jit(solution)/shard_map/all_gather | solution.py:74
  129.1 2.2 gather_fusion
  131.3 0.2 copy.40
  131.5 0.5 fusion.18
  132.1 0.3 fusion.50
  132.4 0.6 copy-done.10
  133.0 0.3 convolution_bitcast_fusion.2
  133.4 0.2 copy.48
  133.8 2.3 convolution_bitcast_fusion.3
  136.0 0.2 copy.46
  136.5 2.5 broadcast_in_dim.53
  139.0 2.6 scatter_fusion
  141.6 1.1 copy-done.11
  142.8 0.7 convolution_convert_fusion.1
  143.5 0.3 convolution_convert_fusion.4
  143.8 0.6 copy-done.2
  144.4 1.3 convolution_bitcast_fusion.1
  145.7 1.3 fusion.39
  147.0 617.3 %reduce-scatter.2.cloned.1.call-done = f32[8,1024]{1,0:T(8,128)} async-done(((f32[1024,1024]{1,0:T(8,128)}), f32[8,1024]{1,0:T(8,128)}) %reduce-scatter.2.cloned.1.call-update) | async-done | bytes 32784 | tf_op jit(solution)/shard_map/reduce_scatter | solution.py:175
  764.4 3.1 convolution_bitcast_fusion
  767.5 1.0 copy-done.9
  768.5 0.4 fusion.7
  769.0 6.0 collective-permute-start
  774.9 1.1 convolution_convert_fusion
  776.0 0.2 collective-permute-done.1
  776.3 0.7 fusion.29
  776.9 0.9 fusion.8
  777.8 4.0 psum.28
  781.8 329.4 %all-reduce.3.cloned.1.call-done = (f32[512,512]{0,1:T(8,128)}, f32[512,1024]{0,1:T(8,128)}, f32[512,512]{1,0:T(8,128)}) async-done(((f32[512,512]{0,1:T(8,128)}, f32[512,1024]{0,1:T(8,128)}, f32[512,512]{1,0:T(8,128)}), (f32[512,512]{0,1:T(8,128)}, f32[512,1024]{0,1:T(8,128)}, f32[512,512]{1,0:T(8,128)})) %all-reduce.3.cloned.1.call-update) | async-done | bytes 4194320 | tf_op jit(solution)/shard_map/psum | solution.py:184
  1111.2 2.5 copy.49
  1113.7 1.7 fusion.46
  1115.5 1.3 copy.50
  1116.8 1.3 copy.51
  1118.1 1.0 copy.60
  (49 shorter events, 1.3 us)
Async XLA Ops:
  7.2 13.0 %copy-start = (bf16[512,512]{1,0:T(8,128)(2,1)S(1)}, bf16[512,512]{1,0:T(8,128)(2,1)}, u32[]{:S(2)}) copy-start(bf16[512,512]{1,0:T(8,128)(2,1)} %param.11) | copy-start | bytes 1572868
  7.2 14.3 %copy-start.7 = (bf16[2,512]{1,0:T(2,128)(2,1)S(1)}, bf16[2,512]{1,0:T(2,128)(2,1)}, u32[]{:S(2)}) copy-start(bf16[2,512]{1,0:T(2,128)(2,1)} %param.17) | copy-start | bytes 6148
  7.2 122.0 %all-gather.2.cloned.1.call-start = ((), (), s32[]{:S(2)}) async-start(), calls=%async_computation.1 | async-start | bytes 2113536 | tf_op jit(solution)/shard_map/all_gather | solution.py:74
  9.8 24.8 %copy-start.8 = (bf16[512,512]{1,0:T(8,128)(2,1)S(1)}, bf16[512,512]{1,0:T(8,128)(2,1)}, u32[]{:S(2)}) copy-start(bf16[512,512]{1,0:T(8,128)(2,1)} %param.14) | copy-start | bytes 1572868
  10.4 754.0 %reduce-scatter.2.cloned.1.call-start = ((), (), s32[]{:S(2)}) async-start(), calls=%async_computation.2 | async-start | bytes 4227072 | tf_op jit(solution)/shard_map/reduce_scatter | solution.py:175
  11.3 10.1 collective-permute-start.3
  11.4 10.1 collective-permute-start.2
  21.6 5.9 collective-permute-start.5
  26.2 7.2 collective-permute-start.4
  132.1 1.0 copy-start.10
  141.5 1.2 copy-start.11
  141.6 969.7 %all-reduce.3.cloned.1.call-start = ((), (), s32[]{:S(2)}) async-start(), calls=%async_computation.3 | async-start | bytes 8388608 | tf_op jit(solution)/shard_map/psum | solution.py:184
  143.5 1.0 copy-start.2
  143.8 620.6 %copy-start.5 = (bf16[8,512]{1,0:T(8,128)(2,1)S(1)}, bf16[8,512]{1,0:T(8,128)(2,1)}, u32[]{:S(2)}) copy-start(bf16[8,512]{1,0:T(8,128)(2,1)} %param.10) | copy-start | bytes 24580
  767.5 1.0 copy-start.9
  767.5 9.4 copy-start.3
  767.5 9.4 copy-start.4
  767.5 9.4 copy-start.6
  769.0 7.3 collective-permute-start.1
  769.0 7.3 collective-permute-start
  1116.8 1.3 copy-start.1
Sparse Core Ops, SparseCore 0:
  12.2 116.8 all-gather.1
  141.7 622.6 reduce-scatter.1
  771.8 339.3 all-reduce.2
where the time goes:
time: 1130 us
  waiting for transfers between devices  1050 us (93%)
  local copies, waits for them, and re-layouts  21.1 us (2%)
  starting transfers between devices  18.1 us (2%)
  matrix products  16.7 us (1%)
  between operations  14 us (1%)
    reduce_scatter x1, waiting for transfers between devices, per_device(): lax.psum_scatter(return_term, 'tile', scatter_dimension=0, tiled=True)  617 us
    psum x1, waiting for transfers between devices, per_device(): lax.psum((grad_query_local, grad_out_local, pair_local), ('tile', 'basin'))  329 us
    all_gather x1, waiting for transfers between devices, fetch_gauges(): return lax.all_gather(moving, 'tile', axis=0, tiled=True)  94.1 us
  transfers between devices with their start and end apart: 9, of which 6 were waited for; matrix products, arithmetic and copies ran while one was open for 1% of the time, Pallas kernels for 0%

commit v1 on v0

--- a/solution.py
+++ b/solution.py
@@ -71,7 +71,9 @@
 
 
 def fetch_gauges(moving):
-    return lax.all_gather(moving, "tile", axis=0, tiled=True)
+    return jnp.concatenate(
+        lax.all_to_all(jnp.stack([moving] * lax.axis_size("tile")), "tile", 0, 0), axis=0
+    )
 
 
 def sum_cores(partial_value):

time: 1130 us -> 1080 us (0.956)
  waiting for transfers between devices: 1050 us -> 992 us
  starting transfers between devices: 18.1 us -> 31.2 us
    all_gather x1 -> x0, waiting for transfers between devices: 94.1 us -> none  [fetch_gauges(): return lax.all_gather(moving, 'tile', axis=0, tiled=True)]
    ppermute x6, waiting for transfers between devices: 7.18 us -> 45 us  [shifted(): return lax.ppermute(value, axis, pairs)]
    all_to_all x0 -> x1, starting transfers between devices: none -> 15.6 us  [fetch_gauges(): lax.all_to_all(jnp.stack([moving] * lax.axis_size('tile')), 'tile', 0, 0)]
where the time goes in v1:
time: 1080 us
  waiting for transfers between devices  992 us (92%)
  starting transfers between devices  31.2 us (3%)
  matrix products  20.6 us (2%)
  local copies, waits for them, and re-layouts  20.3 us (2%)
  between operations  14.3 us (1%)
    reduce_scatter x1, waiting for transfers between devices, per_device(): lax.psum_scatter(return_term, 'tile', scatter_dimension=0, tiled=True)  617 us
    psum x1, waiting for transfers between devices, per_device(): lax.psum((grad_query_local, grad_out_local, pair_local), ('tile', 'basin'))  329 us
    ppermute x6, waiting for transfers between devices, shifted(): return lax.ppermute(value, axis, pairs)  45 us
  transfers between devices with their start and end apart: 9, of which 6 were waited for; matrix products, arithmetic and copies ran while one was open for 1% of the time, Pallas kernels for 0%

profile of v1, /device:TPU:8, one launch (start us, length us, event | category | flops | bytes accessed | tf_op | source)
XLA Modules:
  0.0 1083.1 jit_solution(15357050202038501873)
XLA Ops:
  7.2 1.3 convolution_convert_fusion.6
  8.5 1.2 convolution_convert_fusion.7
  9.7 1.6 stack.2
  11.3 15.6 %all-to-all-start = ((bf16[128,8,1024]{2,1,0:T(8,128)(2,1)}), bf16[128,8,1024]{2,1,0:T(8,128)(2,1)S(1)}, u32[]{:S(2)}, u32[]{:S(2)}) async-start(bf16[128,8,1024]{2,1,0:T(8,128)(2,1)} %stack.2), calls=%async_computation | async-start | bytes 4194304 | tf_op jit(solution)/shard_map/all_to_all | solution.py:75
  27.2 6.0 collective-permute-start.2
  33.2 0.3 convolution_convert_fusion.5
  33.5 38.5 %collective-permute-done.3 = f32[2]{0:T(128)S(1)} collective-permute-done((f32[2]{0:T(128)S(1)}, f32[2]{0:T(128)S(1)}, u32[]{:S(2)}, u32[]{:S(2)}) %collective-permute-start.3) | collective-permute-done | bytes 40 | tf_op jit(solution)/shard_map/ppermute | solution.py:15
  72.2 3.4 collective-permute-start.5
  75.8 0.8 copy.41
  76.7 0.3 collective-permute-done.5
  76.9 5.9 collective-permute-done.4
  82.9 1.2 gather_fusion.1
  84.0 1.4 convolution_convert_fusion.2
  85.4 0.1 copy.44
  85.6 0.6 gather_fusion
  86.5 1.5 fusion.18
  88.0 0.3 fusion.50
  88.4 0.6 copy-done.13
  89.0 0.3 convolution_bitcast_fusion.2
  89.3 0.2 copy.49
  89.5 0.1 concatenate.20
  89.7 0.2 copy-done.6
  89.9 2.3 convolution_bitcast_fusion.3
  92.2 0.2 copy.47
  92.4 0.1 concatenate.19
  92.6 2.5 broadcast_in_dim.53
  95.1 2.6 scatter_fusion
  97.7 0.2 all-reduce.3.cloned.1.call-start
  97.9 2.3 convolution_convert_fusion.1
  100.3 1.6 convolution_convert_fusion.4
  101.9 1.3 convolution_bitcast_fusion.1
  103.1 1.3 fusion.39
  104.5 617.0 %reduce-scatter.2.cloned.1.call-done = f32[8,1024]{1,0:T(8,128)} async-done(((f32[1024,1024]{1,0:T(8,128)}), f32[8,1024]{1,0:T(8,128)}) %reduce-scatter.2.cloned.1.call-update) | async-done | bytes 32784 | tf_op jit(solution)/shard_map/reduce_scatter | solution.py:177
  721.5 3.1 convolution_bitcast_fusion
  724.7 1.0 copy-done.11
  725.7 0.4 fusion.7
  726.1 6.0 collective-permute-start
  732.1 1.1 convolution_convert_fusion
  733.1 0.2 collective-permute-done.1
  733.4 0.7 fusion.29
  734.1 0.9 fusion.8
  735.0 4.0 psum.28
  738.9 329.5 %all-reduce.3.cloned.1.call-done = (f32[512,512]{0,1:T(8,128)}, f32[512,1024]{0,1:T(8,128)}, f32[512,512]{1,0:T(8,128)}) async-done(((f32[512,512]{0,1:T(8,128)}, f32[512,1024]{0,1:T(8,128)}, f32[512,512]{1,0:T(8,128)}), (f32[512,512]{0,1:T(8,128)}, f32[512,1024]{0,1:T(8,128)}, f32[512,512]{1,0:T(8,128)})) %all-reduce.3.cloned.1.call-update) | async-done | bytes 4194320 | tf_op jit(solution)/shard_map/psum | solution.py:186
  1068.4 2.5 copy.50
  1070.9 1.7 fusion.46
  1072.6 1.3 copy.51
  1074.0 1.3 copy.52
  1075.3 1.0 copy.61
  (54 shorter events, 1.2 us)
Async XLA Ops:
  7.2 26.1 %copy-start = (bf16[512,512]{1,0:T(8,128)(2,1)S(1)}, bf16[512,512]{1,0:T(8,128)(2,1)}, u32[]{:S(2)}) copy-start(bf16[512,512]{1,0:T(8,128)(2,1)} %param.11) | copy-start | bytes 1572868
  11.3 15.7 %copy-start.10 = (s32[256]{0:T(256)S(1)}, s32[256]{0:T(256)}, u32[]{:S(2)}) copy-start(s32[256]{0:T(256)} %param.16) | copy-start | bytes 3076
  11.3 21.9 %copy-start.12 = (s32[1,16]{1,0:T(1,128)S(1)}, s32[1,16]{1,0:T(1,128)}, u32[]{:S(2)}) copy-start(s32[1,16]{1,0:T(1,128)} %param.15) | copy-start | bytes 196
  11.3 21.9 %copy-start.2 = (bf16[256,512]{1,0:T(8,128)(2,1)S(1)}, bf16[256,512]{1,0:T(8,128)(2,1)}, u32[]{:S(2)}) copy-start(bf16[256,512]{1,0:T(8,128)(2,1)} %param.9) | copy-start | bytes 786436
  11.3 60.8 %copy-start.9 = (bf16[2,512]{1,0:T(2,128)(2,1)S(1)}, bf16[2,512]{1,0:T(2,128)(2,1)}, u32[]{:S(2)}) copy-start(bf16[2,512]{1,0:T(2,128)(2,1)} %param.17) | copy-start | bytes 6148
  11.3 74.2 %all-to-all-start = ((bf16[128,8,1024]{2,1,0:T(8,128)(2,1)}), bf16[128,8,1024]{2,1,0:T(8,128)(2,1)S(1)}, u32[]{:S(2)}, u32[]{:S(2)}) async-start(bf16[128,8,1024]{2,1,0:T(8,128)(2,1)} %stack.2), calls=%async_computation | async-start | bytes 4194304 | tf_op jit(solution)/shard_map/all_to_all | solution.py:75
  26.9 694.6 %reduce-scatter.2.cloned.1.call-start = ((), (), s32[]{:S(2)}) async-start(), calls=%async_computation.2 | async-start | bytes 4227072 | tf_op jit(solution)/shard_map/reduce_scatter | solution.py:177
  27.2 44.8 %collective-permute-start.3 = (f32[2]{0:T(128)S(1)}, f32[2]{0:T(128)S(1)}, u32[]{:S(2)}, u32[]{:S(2)}) collective-permute-start(f32[2]{0:T(128)S(1)} %get-tuple-element.79), channel_id=1, source_target_pairs={{0,1},{1,2},{2,3},{3,4},{4,5},{5,6},{6,7},{7,8},{8,9},{9,10},{10,1... | collective-permute-start | bytes 32 | tf_op jit(solution)/shard_map/ppermute | solution.py:15
  27.2 44.8 %collective-permute-start.2 = (f32[2]{0:T(128)S(1)}, f32[2]{0:T(128)S(1)}, u32[]{:S(2)}, u32[]{:S(2)}) collective-permute-start(f32[2]{0:T(128)S(1)} %get-tuple-element.78), channel_id=1, source_target_pairs={{0,255},{1,0},{2,1},{3,2},{4,3},{5,4},{6,5},{7,6},{8,7},{9,8},{10,... | collective-permute-start | bytes 32 | tf_op jit(solution)/shard_map/ppermute | solution.py:15
  72.2 4.7 collective-permute-start.5
  75.6 7.2 collective-permute-start.4
  88.0 1.0 copy-start.13
  89.0 0.9 copy-start.6
  97.7 970.7 %all-reduce.3.cloned.1.call-start = ((), (), s32[]{:S(2)}) async-start(), calls=%async_computation.3 | async-start | bytes 8388608 | tf_op jit(solution)/shard_map/psum | solution.py:186
  100.2 1.6 copy-start.3
  101.9 619.7 %copy-start.7 = (bf16[8,512]{1,0:T(8,128)(2,1)S(1)}, bf16[8,512]{1,0:T(8,128)(2,1)}, u32[]{:S(2)}) copy-start(bf16[8,512]{1,0:T(8,128)(2,1)} %param.10) | copy-start | bytes 24580
  724.6 1.0 copy-start.11
  724.6 9.4 copy-start.4
  724.6 9.4 copy-start.5
  724.6 9.4 copy-start.8
  726.1 7.3 collective-permute-start.1
  726.1 7.3 collective-permute-start
  1073.9 1.3 copy-start.1
Sparse Core Ops, SparseCore 0:
  97.8 623.6 reduce-scatter.1
  728.9 339.4 all-reduce.2
